TPU v7x, 256 devices: a whole 4x4x8 slice. The times are simulated.
256 devices in a mesh: row: 8 (over x, core), col: 32 (over y, z).
Axes of the slice: x: 4, y: 4, z: 8, core: 2. Of those that a mesh axis runs over, the one named last changes fastest.
Arguments:
- hidden: bfloat16 [4096, 8192], P('row', 'col'), may hold values from -600 to 600
- norm_gain: float32 [8192], replicated, may hold values from 0.5 to 2
- wq: bfloat16 [8192, 8192], P('row', 'col'), may hold values from -1 to 1
- wk: bfloat16 [8192, 1024], P('row', 'col'), may hold values from -1 to 1
- wv: bfloat16 [8192, 1024], P('row', 'col'), may hold values from -0.0625 to 0.0625
- wo: bfloat16 [8192, 8192], P('row', 'col'), may hold values from -0.25 to 0.25
Outputs:
- attn_out: bfloat16 [4096, 8192], P('row', 'col')
All inputs are finite; a program needn't handle non-finite values.
Results may differ from a plain program's by a relative error of at most 0.011.
Values may be sent and summed in bfloat16 or wider, within the bound.
A program may use at most 64 MiB of HBM per device.

v0:
```python
import jax
import jax.numpy as jnp
from jax import lax
from jax.sharding import PartitionSpec as P

HD = 128


def partner(array, axis, distance):
    return lax.ppermute(array, axis, [(i, i ^ 1 << distance) for i in range(lax.axis_size(axis))])


def rotary(field, positions):
    half = field.shape[-1] // 2
    steps = jnp.arange(half).astype(jnp.float32)
    freqs = 10000.0 ** (-steps / half)
    angles = positions.astype(jnp.float32)[:, None] * freqs[None, :]
    cosine = jnp.cos(angles)[:, None, :]
    sine = jnp.sin(angles)[:, None, :]
    first = field[..., :half]
    second = field[..., half:]
    return jnp.concatenate(
        [first * cosine - second * sine, second * cosine + first * sine], axis=-1
    )


def order_pair(mine, other, col_index, bit, axis_dim):
    upper = col_index // 2**bit % 2 == 1
    lower_part = jnp.where(upper, other, mine)
    upper_part = jnp.where(upper, mine, other)
    return jnp.concatenate([lower_part, upper_part], axis=axis_dim)


def per_device(hidden, norm_gain, wq, wk, wv, wo):
    tok_rows = hidden.shape[0]
    panel = lax.all_gather(hidden, "col", axis=1, tiled=True)
    values_in = panel.astype(jnp.float32)
    meansq = jnp.mean(values_in * values_in, axis=1, keepdims=True)
    normed = (values_in * lax.rsqrt(meansq + 1e-05) * norm_gain).astype(jnp.bfloat16)
    kv_cols = wk.shape[1]
    group = max(1, HD // kv_cols)
    bits = group.bit_length() - 1
    col_index = lax.axis_index("col")
    stacked = jnp.stack((wk, wv), axis=1)
    for bit in range(bits):
        other = partner(stacked, "col", bit)
        stacked = order_pair(stacked, other, col_index, bit, 2)
    columns = normed
    query_part = jnp.dot(
        columns, lax.all_gather(wq, "row", axis=0, tiled=True), preferred_element_type=jnp.float32
    )
    pair_part = jnp.einsum(
        "ho,omr->hmr",
        columns,
        lax.all_gather(stacked, "row", axis=0, tiled=True),
        preferred_element_type=jnp.float32,
    )
    heads_here = wq.shape[1] // HD
    kv_here = pair_part.shape[2] // HD
    per_kv = heads_here // kv_here
    positions = lax.axis_index("row") * tok_rows + jnp.arange(tok_rows)
    queries = rotary(query_part.reshape(tok_rows, heads_here, HD), positions).astype(jnp.bfloat16)
    queries = queries.reshape(tok_rows, kv_here, per_kv, HD)
    keys = rotary(pair_part[:, 0].reshape(tok_rows, kv_here, HD), positions).astype(jnp.bfloat16)
    values = pair_part[:, 1].reshape(tok_rows, kv_here, HD).astype(jnp.bfloat16)
    scale = HD ** (-0.5)
    best = jnp.full((kv_here, per_kv, tok_rows), -1e30, jnp.float32)
    key_piece = lax.all_gather(keys, "row", axis=0, tiled=True)
    value_piece = lax.all_gather(values, "row", axis=0, tiled=True)
    count = key_piece.shape[0]
    scores = (
        jnp.einsum("tagd,nad->agtn", queries, key_piece, preferred_element_type=jnp.float32) * scale
    )
    key_pos = jnp.arange(count)
    visible = positions[:, None] >= key_pos[None, :]
    scores = jnp.where(visible, scores, -jnp.inf)
    fresh = jnp.maximum(best, jnp.max(scores, axis=3))
    probs = jnp.exp(scores - fresh[..., None])
    total = jnp.sum(probs, axis=3)
    update = jnp.einsum(
        "agtn,nad->agtd",
        probs.astype(jnp.bfloat16),
        value_piece,
        preferred_element_type=jnp.float32,
    )
    numer = update
    best, total, numer = (fresh, total, numer)
    heads = (
        (numer / total[..., None])
        .transpose(2, 0, 1, 3)
        .reshape(tok_rows, heads_here * HD)
        .astype(jnp.bfloat16)
    )
    head_panel = lax.all_gather(heads, "col", axis=1, tiled=True)
    columns = head_panel
    result = jnp.dot(
        columns, lax.all_gather(wo, "row", axis=0, tiled=True), preferred_element_type=jnp.float32
    )
    return result.astype(jnp.bfloat16)


def solution(mesh):
    in_specs = (
        P("row", "col"),
        P(),
        P("row", "col"),
        P("row", "col"),
        P("row", "col"),
        P("row", "col"),
    )
    out_specs = P("row", "col")
    return jax.shard_map(
        per_device, mesh=mesh, in_specs=in_specs, out_specs=out_specs, check_vma=False
    )
```

profile of v0, /device:TPU:1, one launch (start us, length us, event | category | flops | bytes accessed | tf_op | source)
XLA Modules:
  0.0 396.9 jit_solution(9538606364416327431)
XLA Ops:
  6.5 0.7 all-gather.8.cloned.1.call-update
  7.3 0.9 pad_maximum_fusion.2
  8.2 2.6 collective-permute-start
  10.7 2.4 collective-permute-done
  13.1 0.9 broadcast_select_fusion.3
  14.0 3.8 collective-permute-start.1
  17.9 11.3 %collective-permute-done.1 = bf16[1024,2,64]{0,2,1:T(8,128)(2,1)S(1)} collective-permute-done((bf16[1024,2,64]{0,2,1:T(8,128)(2,1)S(1)}, bf16[1024,2,64]{0,2,1:T(8,128)(2,1)S(1)}, u32[]{:S(2)}, u32[]{:S(2)}) %collective-permute-start.1) | collective-permute-done | bytes 262176 | tf_op jit(solution)/shard_map/ppermute | solution.py:10
  29.3 0.8 pad_maximum_fusion
  30.2 0.7 all-gather.14.cloned.1.call-update
  31.0 86.2 %all-gather.8.cloned.1.call-done = bf16[512,8192]{1,0:T(8,128)(2,1)} async-done(((bf16[512,256]{1,0:T(8,128)(2,1)}), bf16[512,8192]{1,0:T(8,128)(2,1)}) %all-gather.8.cloned.1.call-update) | async-done | bytes 8388624 | tf_op jit(solution)/shard_map/all_gather | solution.py:36
  117.1 5.1 %fusion = f32[512]{0:T(512)S(1)} fusion(bf16[512,8192]{1,0:T(8,128)(2,1)} %all-gather.8.cloned.1.call-done), kind=kLoop, calls=%fused_computation.2 | loop fusion | flops 12582400 | bytes 8390656 | tf_op jit(solution)/shard_map/reduce_sum | solution.py:38
  122.3 31.8 %all-gather.10.cloned.1.call-done = bf16[8192,2,128]{0,2,1:T(8,128)(2,1)} async-done(((bf16[1024,2,128]{0,2,1:T(8,128)(2,1)}), bf16[8192,2,128]{0,2,1:T(8,128)(2,1)}) %all-gather.10.cloned.1.call-update) | async-done | bytes 4194320 | tf_op jit(solution)/shard_map/all_gather | solution.py:55
  154.1 7.0 %fusion.12 = f32[512,256]{0,1:S(1)} fusion(bf16[8192,256]{0,1:T(8,128)(2,1)} %bitcast.61, bf16[512,8192]{1,0:T(8,128)(2,1)} %all-gather.8.cloned.1.call-done, f32[8192]{0:T(1024)S(1)} %copy-done.1, f32[512]{0:T(512)S(1)} %add_rsqrt_fusion), kind=kOutput, calls=%fused_computation.15 | convolution fusion | flops 2164260864 | bytes 13142016
  161.1 0.6 fusion.35
  161.7 0.7 pad_maximum_fusion.3
  162.4 0.7 slice.34
  163.2 0.5 all-gather.20.cloned.1.call-update
  163.7 0.2 all-gather.18.cloned.1.call-start
  163.9 1.8 multiply_cosine_fusion
  165.7 1.7 iota_compare_fusion
  167.5 23.2 %all-gather.14.cloned.1.call-done = bf16[8192,256]{1,0:T(8,128)(2,1)} async-done(((bf16[1024,256]{1,0:T(8,128)(2,1)}), bf16[8192,256]{1,0:T(8,128)(2,1)}) %all-gather.14.cloned.1.call-update) | async-done | bytes 4194320 | tf_op jit(solution)/shard_map/all_gather | solution.py:50
  190.6 7.6 %fusion.10 = f32[512,256]{0,1:T(8,128)S(1)} fusion(bf16[8192,256]{1,0:T(8,128)(2,1)} %all-gather.14.cloned.1.call-done, bf16[512,8192]{1,0:T(8,128)(2,1)} %all-gather.8.cloned.1.call-done, f32[8192]{0:T(1024)S(1)} %copy-done.1, f32[512]{0:T(512)S(1)} %add_rsqrt_fusion), kind=kOutput, calls=%fused_computation.14 | convolution fusion | flops 2164260864 | bytes 13142016 | tf_op jit(solution)/shard_map/dot_general | solution.py:49
  198.7 1.9 subtract_convert_fusion
  200.5 17.7 %all-gather.12.cloned.1.call-done = bf16[4096,1,128]{0,2,1:T(8,128)(2,1)} async-done(((bf16[512,1,128]{0,2,1:T(8,128)(2,1)}), bf16[4096,1,128]{0,2,1:T(8,128)(2,1)}) %all-gather.12.cloned.1.call-update) | async-done | bytes 1048592 | tf_op jit(solution)/shard_map/all_gather | solution.py:68
  218.2 5.1 %fusion.5 = (f32[2,512]{1,0:T(2,128)S(1)}, f32[4096,512,2]{1,0,2:T(8,128)S(1)}) fusion(pred[512,4096]{0,1:T(8,128)(4,1)S(1)} %iota_compare_fusion, bf16[512,2,64]{2,0,1:T(8,128)(2,1)} %get-tuple-element.6, bf16[512,2,64]{2,0,1:T(8,128)(2,1)S(1)} %get-tuple-element.5, bf16[4096,1,128]{0,2,1:T(8,128)(2,1)} %all-gather.12.cloned.1.call-done), kind=kOutput, calls=%fused_computation.9 | convolution fusion | flops 1086848000 | bytes 20189184 | tf_op jit(solution)/shard_map/tagd,nad->agtn/dot_general | solution.py:72
  223.3 5.7 %copy-done = f32[4096,512,2]{1,0,2:T(8,128)} copy-done((f32[4096,512,2]{1,0,2:T(8,128)}, f32[4096,512,2]{1,0,2:T(8,128)S(1)}, u32[]{:S(2)}) %copy-start) | copy-done | bytes 16777240
  229.0 4.2 %fusion.3 = f32[2,512]{1,0:T(2,128)S(1)} fusion(f32[4096,512,2]{1,0,2:T(8,128)S(1)} %get-tuple-element.18, f32[2,512]{1,0:T(2,128)S(1)} %broadcast_maximum_fusion, pred[512,4096]{0,1:T(8,128)(4,1)S(1)} %iota_compare_fusion), kind=kLoop, calls=%fused_computation.7 | loop fusion | flops 16776192 | bytes 18882560 | tf_op jit(solution)/shard_map/reduce_sum | solution.py:79
  233.2 12.6 %all-gather.16.cloned.1.call-done = bf16[4096,1,128]{0,2,1:T(8,128)(2,1)} async-done(((bf16[512,1,128]{0,2,1:T(8,128)(2,1)}), bf16[4096,1,128]{0,2,1:T(8,128)(2,1)}) %all-gather.16.cloned.1.call-update) | async-done | bytes 1048592 | tf_op jit(solution)/shard_map/all_gather | solution.py:69
  245.8 11.7 %fusion.22 = bf16[2,512,128]{1,2,0:T(8,128)(2,1)} fusion(f32[4096,512,2]{1,0,2:T(8,128)} %copy-done, f32[2,512]{1,0:T(2,128)S(1)} %broadcast_maximum_fusion, pred[512,4096]{0,1:T(8,128)(4,1)S(1)} %iota_compare_fusion, bf16[4096,1,128]{0,2,1:T(8,128)(2,1)} %all-gather.16.cloned.1.call-done, f32[2,512]{1,0:T(2,128)S(1)} %fusion.3), kind=kOutput, calls=%fused_computation.21 | convolution fusion | flops 1090781184 | bytes 20193280 | tf_op jit(solution)/shard_map/agtn,nad->agtd/dot_general | solution.py:80
  257.4 24.6 %all-gather.20.cloned.1.call-done = bf16[8192,256]{1,0:T(8,128)(2,1)} async-done(((bf16[1024,256]{1,0:T(8,128)(2,1)}), bf16[8192,256]{1,0:T(8,128)(2,1)}) %all-gather.20.cloned.1.call-update) | async-done | bytes 4194320 | tf_op jit(solution)/shard_map/all_gather | solution.py:97
  282.0 100.3 %all-gather.18.cloned.1.call-done = bf16[512,8192]{0,1:T(8,128)(2,1)} async-done(((bf16[512,256]{0,1:T(8,128)(2,1)}), bf16[512,8192]{0,1:T(8,128)(2,1)}) %all-gather.18.cloned.1.call-update) | async-done | bytes 8388624 | tf_op jit(solution)/shard_map/all_gather | solution.py:94
  382.4 7.7 %convolution_convert_fusion = bf16[512,256]{1,0:T(8,128)(2,1)} fusion(bf16[512,8192]{0,1:T(8,128)(2,1)} %all-gather.18.cloned.1.call-done, bf16[8192,256]{1,0:T(8,128)(2,1)} %all-gather.20.cloned.1.call-done), kind=kOutput, calls=%fused_computation.16 | convolution fusion | flops 2147614720 | bytes 12845056 | tf_op jit(solution)/shard_map/dot_general | solution.py:96
  (23 shorter events, 0.9 us)
Async XLA Ops:
  6.5 147.6 %copy-start.1 = (f32[8192]{0:T(1024)S(1)}, f32[8192]{0:T(1024)}, u32[]{:S(2)}) copy-start(f32[8192]{0:T(1024)} %param.7) | copy-start | bytes 98308
  6.5 110.6 %all-gather.8.cloned.1.call-start = ((), (), s32[]{:S(2)}) async-start(), calls=%async_computation | async-start | bytes 8650752 | tf_op jit(solution)/shard_map/all_gather | solution.py:36
  7.3 146.8 %all-gather.10.cloned.1.call-start = ((), (), s32[]{:S(2)}) async-start(), calls=%async_computation.1 | async-start | bytes 4718592 | tf_op jit(solution)/shard_map/all_gather | solution.py:55
  8.2 4.9 %collective-permute-start = (bf16[1024,2,32]{0,2,1:T(8,128)(2,1)S(1)}, bf16[1024,2,32]{0,2,1:T(8,128)(2,1)S(1)}, u32[]{:S(2)}, u32[]{:S(2)}) collective-permute-start(bf16[1024,2,32]{0,2,1:T(8,128)(2,1)S(1)} %pad_maximum_fusion.2), channel_id=1, source_target_pairs={{0,1},{1,0},{2,3},{3,2},{4,5},{5,4},{6,7},{7,6},{8,9},{9,8},{10,11... | collective-permute-start | bytes 393224 | tf_op jit(solution)/shard_map/ppermute | solution.py:10
  14.0 15.2 %collective-permute-start.1 = (bf16[1024,2,64]{0,2,1:T(8,128)(2,1)S(1)}, bf16[1024,2,64]{0,2,1:T(8,128)(2,1)S(1)}, u32[]{:S(2)}, u32[]{:S(2)}) collective-permute-start(bf16[1024,2,64]{0,2,1:T(8,128)(2,1)S(1)} %pad_maximum_fusion.1), channel_id=1, source_target_pairs={{0,2},{1,3},{2,0},{3,1},{4,6},{5,7},{6,4},{7,5},{8,10},{9,11},{10,... | collective-permute-start | bytes 786440 | tf_op jit(solution)/shard_map/ppermute | solution.py:10
  30.2 160.5 %all-gather.14.cloned.1.call-start = ((), (), s32[]{:S(2)}) async-start(), calls=%async_computation.3 | async-start | bytes 4718592 | tf_op jit(solution)/shard_map/all_gather | solution.py:50
  30.9 187.3 %all-gather.12.cloned.1.call-start = ((), (), s32[]{:S(2)}) async-start(), calls=%async_computation.2 | async-start | bytes 1179648 | tf_op jit(solution)/shard_map/all_gather | solution.py:68
  162.4 83.4 %all-gather.16.cloned.1.call-start = ((), (), s32[]{:S(2)}) async-start(), calls=%async_computation.4 | async-start | bytes 1179648 | tf_op jit(solution)/shard_map/all_gather | solution.py:69
  163.1 118.9 %all-gather.20.cloned.1.call-start = ((), (), s32[]{:S(2)}) async-start(), calls=%async_computation.6 | async-start | bytes 4718592 | tf_op jit(solution)/shard_map/all_gather | solution.py:97
  163.7 218.7 %all-gather.18.cloned.1.call-start = ((), (), s32[]{:S(2)}) async-start(), calls=%async_computation.5 | async-start | bytes 8650752 | tf_op jit(solution)/shard_map/all_gather | solution.py:94
  223.3 5.7 %copy-start = (f32[4096,512,2]{1,0,2:T(8,128)}, f32[4096,512,2]{1,0,2:T(8,128)S(1)}, u32[]{:S(2)}) copy-start(f32[4096,512,2]{1,0,2:T(8,128)S(1)} %get-tuple-element.18) | copy-start | bytes 50331652
Sparse Core Ops, SparseCore 0:
  9.8 107.2 all-gather.7
  119.0 35.0 all-gather.9
  156.0 34.6 all-gather.13
  192.3 25.8 all-gather.11
  219.9 25.7 all-gather.15
  247.5 34.5 all-gather.19
  284.6 97.6 all-gather.17
where the time goes:
time: 397 us
  waiting for transfers between devices  312 us (79%)
  matrix products  39 us (10%)
  other arithmetic  18.7 us (5%)
  between operations  13.6 us (3%)
  local copies, waits for them, and re-layouts  6.8 us (2%)
  starting transfers between devices  6.8 us (2%)
    all_gather x1, waiting for transfers between devices, per_device(): head_panel = lax.all_gather(heads, 'col', axis=1, tiled=True)  100 us
    all_gather x1, waiting for transfers between devices, per_device(): panel = lax.all_gather(hidden, 'col', axis=1, tiled=True)  86.2 us
    all_gather x1, waiting for transfers between devices, per_device(): lax.all_gather(stacked, 'row', axis=0, tiled=True)  31.8 us
    all_gather x1, waiting for transfers between devices, per_device(): lax.all_gather(wo, 'row', axis=0, tiled=True)  24.6 us
    all_gather x1, waiting for transfers between devices, per_device(): lax.all_gather(wq, 'row', axis=0, tiled=True)  23.2 us
    all_gather x1, waiting for transfers between devices, per_device(): key_piece = lax.all_gather(keys, 'row', axis=0, tiled=True)  17.7 us
    ppermute x2, waiting for transfers between devices, partner(): lax.ppermute(array, axis, [(i, i ^ 1 << distance) for i in range(lax.axis...  13.7 us
    all_gather x1, waiting for transfers between devices, per_device(): value_piece = lax.all_gather(values, 'row', axis=0, tiled=True)  12.6 us
  transfers between devices with their start and end apart: 9, of which 9 were waited for; matrix products, arithmetic and copies ran while one was open for 13% of the time, Pallas kernels for 0%

commit v1 on v0

--- a/solution.py
+++ b/solution.py
@@ -66,7 +66,12 @@
     scale = HD ** (-0.5)
     best = jnp.full((kv_here, per_kv, tok_rows), -1e30, jnp.float32)
     key_piece = lax.all_gather(keys, "row", axis=0, tiled=True)
-    value_piece = lax.all_gather(values, "row", axis=0, tiled=True)
+    ring = [values]
+    for hop in range(7):
+        ring.append(lax.ppermute(ring[-1], "row", [(dev, (dev + 1) % 8) for dev in range(8)]))
+    value_piece = jnp.roll(
+        jnp.concatenate(ring[::-1], axis=0), (lax.axis_index("row") + 1) * ring[0].shape[0], axis=0
+    )
     count = key_piece.shape[0]
     scores = (
         jnp.einsum("tagd,nad->agtn", queries, key_piece, preferred_element_type=jnp.float32) * scale

time: 397 us -> 374 us (0.942)
  waiting for transfers between devices: 312 us -> 279 us
  starting transfers between devices: 6.8 us -> 17.3 us
  matrix products: 39 us -> 34.4 us
  local copies, waits for them, and re-layouts: 6.8 us -> 11.4 us
    all_gather x1, waiting for transfers between devices: 17.7 us -> 1.25 us  [per_device(): key_piece = lax.all_gather(keys, 'row', axis=0, tiled=True)]
    ppermute x0 -> x7, waiting for transfers between devices: none -> 15.5 us  [per_device(): lax.ppermute(ring[-1], 'row', [(dev, (dev + 1) % 8) for dev in range(8)])]
    all_gather x1, waiting for transfers between devices: 23.2 us -> 8.27 us  [per_device(): lax.all_gather(wq, 'row', axis=0, tiled=True)]
    all_gather x1 -> x0, waiting for transfers between devices: 12.6 us -> none  [per_device(): value_piece = lax.all_gather(values, 'row', axis=0, tiled=True)]
    ppermute x0 -> x7, starting transfers between devices: none -> 10.7 us  [per_device(): lax.ppermute(ring[-1], 'row', [(dev, (dev + 1) % 8) for dev in range(8)])]
    dot_general x1, matrix products: 11.7 us -> 6.44 us  [per_device(): jnp.einsum('agtn,nad->agtd', probs.astype(jnp.bfloat16), value_piece, pre...]
    unnamed x6 -> x21, local copies, waits for them, and re-layouts: 6.1 us -> 10.7 us
    all_gather x1, waiting for transfers between devices: 24.6 us -> 20.4 us  [per_device(): lax.all_gather(wo, 'row', axis=0, tiled=True)]
  transfers between devices with their start and end apart: 9 -> 15, of which waited for: 9 -> 14; matrix products, arithmetic and copies ran while one was open for 13% -> 15% of each run, Pallas kernels for 0% -> 0%
where the time goes in v1:
time: 374 us; the launch traced here: 373 us
  waiting for transfers between devices  279 us (75%)
  matrix products  34.4 us (9%)
  other arithmetic  17.9 us (5%)
  starting transfers between devices  17.3 us (5%)
  between operations  13.7 us (4%)
  local copies, waits for them, and re-layouts  11.4 us (3%)
    all_gather x1, waiting for transfers between devices, per_device(): head_panel = lax.all_gather(heads, 'col', axis=1, tiled=True)  100 us
    all_gather x1, waiting for transfers between devices, per_device(): panel = lax.all_gather(hidden, 'col', axis=1, tiled=True)  86.1 us
    all_gather x1, waiting for transfers between devices, per_device(): lax.all_gather(stacked, 'row', axis=0, tiled=True)  31.8 us
    all_gather x1, waiting for transfers between devices, per_device(): lax.all_gather(wo, 'row', axis=0, tiled=True)  20.4 us
    ppermute x7, waiting for transfers between devices, per_device(): lax.ppermute(ring[-1], 'row', [(dev, (dev + 1) % 8) for dev in range(8)])  15.5 us
    ppermute x2, waiting for transfers between devices, partner(): lax.ppermute(array, axis, [(i, i ^ 1 << distance) for i in range(lax.axis...  13.7 us
    ppermute x7, starting transfers between devices, per_device(): lax.ppermute(ring[-1], 'row', [(dev, (dev + 1) % 8) for dev in range(8)])  10.7 us
    unnamed x21, local copies, waits for them, and re-layouts  10.7 us
  transfers between devices with their start and end apart: 15, of which 14 were waited for; matrix products, arithmetic and copies ran while one was open for 15% of the time, Pallas kernels for 0%

profile of v1, /device:TPU:1, one launch (start us, length us, event | category | flops | bytes accessed | tf_op | source)
XLA Modules:
  0.0 373.4 jit_solution(7736142410809775746)
XLA Ops:
  7.3 0.9 pad_maximum_fusion.2
  8.2 2.6 collective-permute-start
  10.7 2.4 collective-permute-done
  13.1 0.9 broadcast_select_fusion.3
  14.0 3.8 %collective-permute-start.1 = (bf16[1024,2,64]{0,2,1:T(8,128)(2,1)S(1)}, bf16[1024,2,64]{0,2,1:T(8,128)(2,1)S(1)}, u32[]{:S(2)}, u32[]{:S(2)}) collective-permute-start(bf16[1024,2,64]{0,2,1:T(8,128)(2,1)S(1)} %pad_maximum_fusion.1), channel_id=1, source_target_pairs={{0,2},{1,3},{2,0},{3,1},{4,6},{5,7},{6,4},{7,5},{8,10},{9,11},{10,... | collective-permute-start | bytes 786440 | tf_op jit(solution)/shard_map/ppermute | solution.py:10
  17.9 11.3 %collective-permute-done.1 = bf16[1024,2,64]{0,2,1:T(8,128)(2,1)S(1)} collective-permute-done((bf16[1024,2,64]{0,2,1:T(8,128)(2,1)S(1)}, bf16[1024,2,64]{0,2,1:T(8,128)(2,1)S(1)}, u32[]{:S(2)}, u32[]{:S(2)}) %collective-permute-start.1) | collective-permute-done | bytes 262176 | tf_op jit(solution)/shard_map/ppermute | solution.py:10
  29.3 0.8 pad_maximum_fusion
  31.0 86.1 %all-gather.7.cloned.1.call-done = bf16[512,8192]{1,0:T(8,128)(2,1)} async-done(((bf16[512,256]{1,0:T(8,128)(2,1)}), bf16[512,8192]{1,0:T(8,128)(2,1)}) %all-gather.7.cloned.1.call-update) | async-done | bytes 8388624 | tf_op jit(solution)/shard_map/all_gather | solution.py:36
  117.1 5.1 %fusion = f32[512]{0:T(512)S(1)} fusion(bf16[512,8192]{1,0:T(8,128)(2,1)} %all-gather.7.cloned.1.call-done), kind=kLoop, calls=%fused_computation.2 | loop fusion | flops 12582400 | bytes 8390656 | tf_op jit(solution)/shard_map/reduce_sum | solution.py:38
  122.3 31.8 %all-gather.9.cloned.1.call-done = bf16[8192,2,128]{0,2,1:T(8,128)(2,1)} async-done(((bf16[1024,2,128]{0,2,1:T(8,128)(2,1)}), bf16[8192,2,128]{0,2,1:T(8,128)(2,1)}) %all-gather.9.cloned.1.call-update) | async-done | bytes 4194320 | tf_op jit(solution)/shard_map/all_gather | solution.py:55
  154.1 7.0 %fusion.12 = f32[512,256]{0,1:S(1)} fusion(bf16[8192,256]{0,1:T(8,128)(2,1)} %bitcast.63, bf16[512,8192]{1,0:T(8,128)(2,1)} %all-gather.7.cloned.1.call-done, f32[8192]{0:T(1024)S(1)} %copy-done.1, f32[512]{0:T(512)S(1)} %add_rsqrt_fusion), kind=kOutput, calls=%fused_computation.15 | convolution fusion | flops 2164260864 | bytes 13142016
  162.8 1.9 collective-permute-done.2
  164.7 2.4 collective-permute-start.3
  167.3 2.3 collective-permute-done.3
  169.6 2.6 collective-permute-start.4
  172.2 3.0 iota_compare_fusion
  175.3 2.1 collective-permute-done.4
  177.4 2.0 collective-permute-start.5
  179.4 1.0 multiply_cosine_fusion
  180.4 5.4 %collective-permute-done.5 = bf16[512,1,128]{0,2,1:T(8,128)(2,1)S(1)} collective-permute-done((bf16[512,1,128]{0,2,1:T(8,128)(2,1)S(1)}, bf16[512,1,128]{0,2,1:T(8,128)(2,1)S(1)}, u32[]{:S(2)}, u32[]{:S(2)}) %collective-permute-start.5) | collective-permute-done | bytes 131104 | tf_op jit(solution)/shard_map/ppermute | solution.py:71
  186.6 8.3 %all-gather.13.cloned.1.call-done = bf16[8192,256]{1,0:T(8,128)(2,1)} async-done(((bf16[1024,256]{1,0:T(8,128)(2,1)}), bf16[8192,256]{1,0:T(8,128)(2,1)}) %all-gather.13.cloned.1.call-update) | async-done | bytes 4194320 | tf_op jit(solution)/shard_map/all_gather | solution.py:50
  194.8 7.6 %fusion.10 = f32[512,256]{0,1:T(8,128)S(1)} fusion(bf16[8192,256]{1,0:T(8,128)(2,1)} %all-gather.13.cloned.1.call-done, bf16[512,8192]{1,0:T(8,128)(2,1)} %all-gather.7.cloned.1.call-done, f32[8192]{0:T(1024)S(1)} %copy-done.1, f32[512]{0:T(512)S(1)} %add_rsqrt_fusion), kind=kOutput, calls=%fused_computation.14 | convolution fusion | flops 2164260864 | bytes 13142016 | tf_op jit(solution)/shard_map/dot_general | solution.py:49
  202.9 1.5 collective-permute-done.7
  204.4 2.4 collective-permute-start.8
  207.7 2.2 collective-permute-done.8
  220.9 1.3 all-gather.11.cloned.1.call-done
  222.1 5.7 %fusion.5 = (f32[2,512]{1,0:T(2,128)S(1)}, f32[4096,512,2]{1,0,2:T(8,128)S(1)}) fusion(pred[512,4096]{0,1:T(8,128)(4,1)} %iota_compare_fusion, bf16[512,2,64]{2,0,1:T(8,128)(2,1)} %get-tuple-element.6, bf16[512,2,64]{2,0,1:T(8,128)(2,1)S(1)} %get-tuple-element.5, bf16[4096,1,128]{0,2,1:T(8,128)(2,1)} %all-gather.11.cloned.1.call-done), kind=kOutput, calls=%fused_computation.9 | convolution fusion | flops 1086848000 | bytes 20189184 | tf_op jit(solution)/shard_map/tagd,nad->agtn/dot_general | solution.py:77
  227.8 4.0 %fusion.3 = f32[2,512]{1,0:T(2,128)S(1)} fusion(f32[4096,512,2]{1,0,2:T(8,128)S(1)} %get-tuple-element.18, f32[2,512]{1,0:T(2,128)S(1)} %broadcast_maximum_fusion, pred[512,4096]{0,1:T(8,128)(4,1)S(1)} %copy-done), kind=kLoop, calls=%fused_computation.7 | loop fusion | flops 16776192 | bytes 18882560 | tf_op jit(solution)/shard_map/reduce_sum | solution.py:84
  231.8 6.4 %fusion.23 = bf16[2,512,128]{1,2,0:T(8,128)(2,1)} fusion(f32[4096,512,2]{1,0,2:T(8,128)S(1)} %get-tuple-element.18, f32[2,512]{1,0:T(2,128)S(1)} %broadcast_maximum_fusion, pred[512,4096]{0,1:T(8,128)(4,1)} %iota_compare_fusion, bf16[8192,1,128]{0,2,1:T(8,128)(2,1)} %constant_dynamic-update-slice_fusion, s32[]{:T(128)S(6)} %select_n.67, f32[2,512]{1,0:T(2,128)S(1)} %fusion.3), kind=kOutput, calls=%fused_computation.22 | convolution fusion | flops 1090781184 | bytes 20193284 | tf_op jit(solution)/shard_map/agtn,nad->agtd/dot_general | solution.py:85
  238.3 20.4 %all-gather.17.cloned.1.call-done = bf16[8192,256]{1,0:T(8,128)(2,1)} async-done(((bf16[1024,256]{1,0:T(8,128)(2,1)}), bf16[8192,256]{1,0:T(8,128)(2,1)}) %all-gather.17.cloned.1.call-update) | async-done | bytes 4194320 | tf_op jit(solution)/shard_map/all_gather | solution.py:102
  258.7 100.2 %all-gather.15.cloned.1.call-done = bf16[512,8192]{0,1:T(8,128)(2,1)} async-done(((bf16[512,256]{0,1:T(8,128)(2,1)}), bf16[512,8192]{0,1:T(8,128)(2,1)}) %all-gather.15.cloned.1.call-update) | async-done | bytes 8388624 | tf_op jit(solution)/shard_map/all_gather | solution.py:99
  358.9 7.7 %convolution_convert_fusion = bf16[512,256]{1,0:T(8,128)(2,1)} fusion(bf16[512,8192]{0,1:T(8,128)(2,1)} %all-gather.15.cloned.1.call-done, bf16[8192,256]{1,0:T(8,128)(2,1)} %all-gather.17.cloned.1.call-done), kind=kOutput, calls=%fused_computation.16 | convolution fusion | flops 2147614720 | bytes 12845056 | tf_op jit(solution)/shard_map/dot_general | solution.py:101
  (50 shorter events, 16.5 us)
Async XLA Ops:
  6.5 110.6 %all-gather.7.cloned.1.call-start = ((), (), s32[]{:S(2)}) async-start(), calls=%async_computation | async-start | bytes 8650752 | tf_op jit(solution)/shard_map/all_gather | solution.py:36
  7.3 146.8 %all-gather.9.cloned.1.call-start = ((), (), s32[]{:S(2)}) async-start(), calls=%async_computation.1 | async-start | bytes 4718592 | tf_op jit(solution)/shard_map/all_gather | solution.py:55
  8.2 4.9 %collective-permute-start = (bf16[1024,2,32]{0,2,1:T(8,128)(2,1)S(1)}, bf16[1024,2,32]{0,2,1:T(8,128)(2,1)S(1)}, u32[]{:S(2)}, u32[]{:S(2)}) collective-permute-start(bf16[1024,2,32]{0,2,1:T(8,128)(2,1)S(1)} %pad_maximum_fusion.2), channel_id=1, source_target_pairs={{0,1},{1,0},{2,3},{3,2},{4,5},{5,4},{6,7},{7,6},{8,9},{9,8},{10,11... | collective-permute-start | bytes 393224 | tf_op jit(solution)/shard_map/ppermute | solution.py:10
  14.0 15.2 %collective-permute-start.1 = (bf16[1024,2,64]{0,2,1:T(8,128)(2,1)S(1)}, bf16[1024,2,64]{0,2,1:T(8,128)(2,1)S(1)}, u32[]{:S(2)}, u32[]{:S(2)}) collective-permute-start(bf16[1024,2,64]{0,2,1:T(8,128)(2,1)S(1)} %pad_maximum_fusion.1), channel_id=1, source_target_pairs={{0,2},{1,3},{2,0},{3,1},{4,6},{5,7},{6,4},{7,5},{8,10},{9,11},{10,... | collective-permute-start | bytes 786440 | tf_op jit(solution)/shard_map/ppermute | solution.py:10
  30.2 164.7 %all-gather.13.cloned.1.call-start = ((), (), s32[]{:S(2)}) async-start(), calls=%async_computation.3 | async-start | bytes 4718592 | tf_op jit(solution)/shard_map/all_gather | solution.py:50
  30.9 191.2 %all-gather.11.cloned.1.call-start = ((), (), s32[]{:S(2)}) async-start(), calls=%async_computation.2 | async-start | bytes 1179648 | tf_op jit(solution)/shard_map/all_gather | solution.py:68
  31.0 123.1 %copy-start.1 = (f32[8192]{0:T(1024)S(1)}, f32[8192]{0:T(1024)}, u32[]{:S(2)}) copy-start(f32[8192]{0:T(1024)} %param.7) | copy-start | bytes 98308
  162.4 96.4 %all-gather.17.cloned.1.call-start = ((), (), s32[]{:S(2)}) async-start(), calls=%async_computation.5 | async-start | bytes 4718592 | tf_op jit(solution)/shard_map/all_gather | solution.py:102
  162.4 2.3 collective-permute-start.2
  164.7 4.9 %collective-permute-start.3 = (bf16[512,1,128]{0,2,1:T(8,128)(2,1)S(1)}, bf16[512,1,128]{0,2,1:T(8,128)(2,1)S(1)}, u32[]{:S(2)}, u32[]{:S(2)}) collective-permute-start(bf16[512,1,128]{0,2,1:T(8,128)(2,1)S(1)} %collective-permute-done.2), channel_id=1, source_target_pairs={{0,32},{32,64},{64,96},{96,128},{128,160},{160,192},{192,224},{224... | collective-permute-start | bytes 393224 | tf_op jit(solution)/shard_map/ppermute | solution.py:71
  167.2 191.7 %all-gather.15.cloned.1.call-start = ((), (), s32[]{:S(2)}) async-start(), calls=%async_computation.4 | async-start | bytes 8650752 | tf_op jit(solution)/shard_map/all_gather | solution.py:99
  169.6 7.8 %collective-permute-start.4 = (bf16[512,1,128]{0,2,1:T(8,128)(2,1)S(1)}, bf16[512,1,128]{0,2,1:T(8,128)(2,1)S(1)}, u32[]{:S(2)}, u32[]{:S(2)}) collective-permute-start(bf16[512,1,128]{0,2,1:T(8,128)(2,1)S(1)} %collective-permute-done.3), channel_id=1, source_target_pairs={{0,32},{32,64},{64,96},{96,128},{128,160},{160,192},{192,224},{224... | collective-permute-start | bytes 393224 | tf_op jit(solution)/shard_map/ppermute | solution.py:71
  177.4 8.4 %collective-permute-start.5 = (bf16[512,1,128]{0,2,1:T(8,128)(2,1)S(1)}, bf16[512,1,128]{0,2,1:T(8,128)(2,1)S(1)}, u32[]{:S(2)}, u32[]{:S(2)}) collective-permute-start(bf16[512,1,128]{0,2,1:T(8,128)(2,1)S(1)} %collective-permute-done.4), channel_id=1, source_target_pairs={{0,32},{32,64},{64,96},{96,128},{128,160},{160,192},{192,224},{224... | collective-permute-start | bytes 393224 | tf_op jit(solution)/shard_map/ppermute | solution.py:71
  185.8 16.6 %collective-permute-start.6 = (bf16[512,1,128]{0,2,1:T(8,128)(2,1)S(1)}, bf16[512,1,128]{0,2,1:T(8,128)(2,1)S(1)}, u32[]{:S(2)}, u32[]{:S(2)}) collective-permute-start(bf16[512,1,128]{0,2,1:T(8,128)(2,1)S(1)} %collective-permute-done.5), channel_id=1, source_target_pairs={{0,32},{32,64},{64,96},{96,128},{128,160},{160,192},{192,224},{224... | collective-permute-start | bytes 393224 | tf_op jit(solution)/shard_map/ppermute | solution.py:71
  202.4 2.0 collective-permute-start.7
  204.4 5.5 %collective-permute-start.8 = (bf16[512,1,128]{0,2,1:T(8,128)(2,1)S(1)}, bf16[512,1,128]{0,2,1:T(8,128)(2,1)S(1)}, u32[]{:S(2)}, u32[]{:S(2)}) collective-permute-start(bf16[512,1,128]{0,2,1:T(8,128)(2,1)S(1)} %collective-permute-done.7), channel_id=1, source_target_pairs={{0,32},{32,64},{64,96},{96,128},{128,160},{160,192},{192,224},{224... | collective-permute-start | bytes 393224 | tf_op jit(solution)/shard_map/ppermute | solution.py:71
  222.1 5.7 %copy-start = (pred[512,4096]{0,1:T(8,128)(4,1)S(1)}, pred[512,4096]{0,1:T(8,128)(4,1)}, u32[]{:S(2)}) copy-start(pred[512,4096]{0,1:T(8,128)(4,1)} %iota_compare_fusion) | copy-start | bytes 6291460
Sparse Core Ops, SparseCore 0:
  9.8 107.2 all-gather.6
  119.0 35.0 all-gather.8
  156.0 38.8 all-gather.12
  196.5 25.5 all-gather.10
  223.8 34.8 all-gather.16
  261.2 97.6 all-gather.14
